TPU v7x, 128 devices: a whole 4x4x4 slice. The times are simulated.
128 devices in a mesh: dp: 16 (over y, z), mp: 8 (over x, core).
Axes of the slice: x: 4, y: 4, z: 4, core: 2. Of those that a mesh axis runs over, the one named last changes fastest.
Arguments:
- hidden_in: bfloat16 [4096, 2304], P('dp'), may hold values from -6 to 6
- attn_gain: float32 [2304], replicated, may hold values from 0.25 to 1.75
- w_query: bfloat16 [2304, 2048], P(None, 'mp'), may hold values from -0.25 to 0.25
- w_key: bfloat16 [2304, 2048], P(None, 'mp'), may hold values from -0.125 to 0.125
- w_value: bfloat16 [2304, 2048], P(None, 'mp'), may hold values from -0.125 to 0.125
- w_out: bfloat16 [2048, 2304], P('mp'), may hold values from -0.5 to 0.5
- root_cache: bfloat16 [2, 4096, 2048], P(None, 'dp', 'mp'), may hold values from -400 to 400
- mid_cache: bfloat16 [2, 16, 1024, 2048], P(None, 'dp', None, 'mp'), may hold values from -400 to 400
- leaf_cache: bfloat16 [2, 32, 1024, 2048], P(None, 'dp', None, 'mp'), may hold values from -400 to 400
- mid_len: int32 [16], P('dp'), may hold values from 1 to 1024, 8192 in all
- leaf_len: int32 [32], P('dp'), may hold values from 1 to 1024, 16384 in all
- leaf_of: int32 [128], P('dp'), may hold values from 0 to 31, as said below
- parents: int32 [32], replicated, may hold values from 0 to 15, as said below
- suffix_len: int32 [128], P('dp'), may hold values from 1 to 32, 3072 in all
- ffn_gain: float32 [2304], replicated, may hold values from 0.25 to 1.75
- w_router: float32 [2304, 8], replicated, may hold values from -0.5 to 0.5
- routes: int32 [4096, 2], P('dp'), may hold values from 0 to 7, all different within a row; in each aligned block of 256 rows (0 to 255, 256 to 511, ...) at most 96 rows name the same one
- w_gate: bfloat16 [8, 2304, 5760], P('mp', None, 'dp'), may hold values from -0.125 to 0.125
- w_up: bfloat16 [8, 2304, 5760], P('mp', None, 'dp'), may hold values from -0.125 to 0.125
- w_down: bfloat16 [8, 5760, 2304], P('mp', 'dp'), may hold values from -0.078125 to 0.078125
Outputs:
- layer_out: bfloat16 [4096, 2304], P(('dp', 'mp'))
Inputs may be any that keep to these rules, and one draw needn't show every extreme that they name: `leaf_of`: leaf n belongs to index n // 2 of dp, mid-level node n to index n. The 8 sequences of one index of dp have different mid-level nodes and leaves of one parity, so that no two of them share a mid-level node or a leaf's owner. `parents`: every mid-level node is the parent of exactly one even and one odd leaf. `routes`: in the rows of one index of dp no expert is named by more than 96 rows; some indices of dp reach 96.
All inputs are finite; a program needn't handle non-finite values. No bound on the sum of `mid_len` or of `leaf_len` or of `suffix_len` on one device may be relied on, other than what follows from the above.
Results may differ from a plain program's by a relative error of at most 0.015.
The roundings to bfloat16 on the way count: a program that leaves them out, or rounds other values in their place, can miss the bound.
Values may be sent and summed in bfloat16 or wider, within the bound.
A program may use at most 128 MiB of HBM per device.

v0:
```python
import math
import jax
import jax.numpy as jnp
from jax import lax
from jax.sharding import PartitionSpec as P

HD = 64
TOP = 2
EPS = 1e-05
NEGATIVE = -1e30


def rms_scale(rows, gain):
    rows_wide = rows.astype(jnp.float32)
    mean_square = jnp.mean(rows_wide * rows_wide, axis=-1, keepdims=True)
    return rows_wide * lax.rsqrt(mean_square + EPS) * gain


def level_partial(queries, node_keys, node_values, limits, heads_here, batched):
    senders, row_count, width = queries.shape
    head_dim = width // heads_here
    scale = 1.0 / math.sqrt(head_dim)
    query_heads = queries.reshape(senders, row_count, heads_here, head_dim)
    if batched:
        key_heads = node_keys.reshape(senders, -1, heads_here, head_dim)
        value_heads = node_values.reshape(senders, -1, heads_here, head_dim)
        scores = jnp.einsum(
            "sqhd,skhd->sqhk", query_heads, key_heads, preferred_element_type=jnp.float32
        )
    else:
        key_heads = node_keys.reshape(-1, heads_here, head_dim)
        value_heads = node_values.reshape(-1, heads_here, head_dim)
        scores = jnp.einsum(
            "sqhd,khd->sqhk", query_heads, key_heads, preferred_element_type=jnp.float32
        )
    scores = scores * scale
    slots = jnp.arange(scores.shape[-1], dtype=jnp.int32)
    allowed = slots[None, :] < limits[:, None]
    scores = jnp.where(allowed[:, None, None, :], scores, NEGATIVE)
    peak = jnp.max(scores, axis=-1)
    weights = jnp.exp(scores - peak[..., None])
    total = jnp.sum(weights, axis=-1)
    probs = weights.astype(jnp.bfloat16)
    if batched:
        summed = jnp.einsum(
            "sqhk,skhd->sqhd", probs, value_heads, preferred_element_type=jnp.float32
        )
    else:
        summed = jnp.einsum(
            "sqhk,khd->sqhd", probs, value_heads, preferred_element_type=jnp.float32
        )
    result = (summed / total[..., None]).reshape(senders, row_count, width)
    return (result, peak + jnp.log(total))


def on_device(
    hidden_in,
    attn_gain,
    w_query,
    w_key,
    w_value,
    w_out,
    root_cache,
    mid_cache,
    leaf_cache,
    mid_len,
    leaf_len,
    leaf_of,
    parents,
    suffix_len,
    ffn_gain,
    w_router,
    routes,
    w_gate,
    w_up,
    w_down,
):
    tok_rows, width = hidden_in.shape
    seq_rows = suffix_len.shape[0]
    suffix = tok_rows // seq_rows
    head_dim = HD
    local_width = w_query.shape[1]
    heads_here = local_width // head_dim
    scale = 1.0 / math.sqrt(head_dim)
    owners = lax.axis_size("dp")
    normed = rms_scale(hidden_in, attn_gain).astype(jnp.bfloat16)
    query = jnp.dot(normed, w_query, preferred_element_type=jnp.float32).astype(jnp.bfloat16)
    key = jnp.dot(normed, w_key, preferred_element_type=jnp.float32).astype(jnp.bfloat16)
    value = jnp.dot(normed, w_value, preferred_element_type=jnp.float32).astype(jnp.bfloat16)
    query_heads = query.reshape(tok_rows, heads_here, head_dim)
    piece = lax.all_gather(root_cache, "dp", axis=1, tiled=True)
    running_peak = jnp.full((tok_rows, heads_here), NEGATIVE, jnp.float32)
    piece_keys = piece[0].reshape(-1, heads_here, head_dim)
    piece_values = piece[1].reshape(-1, heads_here, head_dim)
    scores = (
        jnp.einsum("qhd,khd->qhk", query_heads, piece_keys, preferred_element_type=jnp.float32)
        * scale
    )
    new_peak = jnp.maximum(running_peak, jnp.max(scores, axis=-1))
    weights = jnp.exp(scores - new_peak[..., None])
    new_total = jnp.sum(weights, axis=-1)
    added = jnp.einsum(
        "qhk,khd->qhd",
        weights.astype(jnp.bfloat16),
        piece_values,
        preferred_element_type=jnp.float32,
    )
    root_out = added / new_total[..., None]
    root_lse = new_peak + jnp.log(new_total)
    query_seq = query.reshape(seq_rows, suffix, heads_here, head_dim)
    key_seq = key.reshape(seq_rows, suffix, heads_here, head_dim)
    value_seq = value.reshape(seq_rows, suffix, heads_here, head_dim)
    slots = jnp.arange(suffix, dtype=jnp.int32)
    self_ok = (slots[None, None, :] <= slots[None, :, None]) & (
        slots[None, None, :] < suffix_len[:, None, None]
    )
    self_scores = (
        jnp.einsum("sqhd,skhd->sqhk", query_seq, key_seq, preferred_element_type=jnp.float32)
        * scale
    )
    self_scores = jnp.where(self_ok[:, :, None, :], self_scores, NEGATIVE)
    self_peak = jnp.max(self_scores, axis=-1)
    self_weights = jnp.exp(self_scores - self_peak[..., None])
    self_total = jnp.sum(self_weights, axis=-1)
    self_sum = jnp.einsum(
        "sqhk,skhd->sqhd",
        self_weights.astype(jnp.bfloat16),
        value_seq,
        preferred_element_type=jnp.float32,
    )
    self_out = (self_sum / self_total[..., None]).reshape(tok_rows, heads_here, head_dim)
    self_lse = (self_peak + jnp.log(self_total)).reshape(tok_rows, heads_here)
    mid_of = parents[leaf_of]
    leaf_owner = leaf_of // 2
    targets = jnp.arange(owners, dtype=jnp.int32)
    pick_mid = (mid_of[None, :] == targets[:, None]).astype(jnp.bfloat16)
    pick_leaf = (leaf_owner[None, :] == targets[:, None]).astype(jnp.bfloat16)
    flat_query = query.reshape(seq_rows, suffix * local_width)
    sent_mid = jnp.dot(pick_mid, flat_query, preferred_element_type=jnp.float32).astype(
        jnp.bfloat16
    )
    sent_leaf = jnp.dot(pick_leaf, flat_query, preferred_element_type=jnp.float32).astype(
        jnp.bfloat16
    )
    sent = jnp.stack([sent_mid, sent_leaf], axis=1).reshape(owners, 2, suffix, local_width)
    sent_queries = lax.all_to_all(sent, "dp", split_axis=0, concat_axis=0, tiled=True)
    leaf_every = lax.all_gather(leaf_of, "dp", axis=0, tiled=True).reshape(owners, seq_rows)
    me_dp = lax.axis_index("dp")
    second = jnp.any((leaf_every // 2 == me_dp) & (leaf_every % 2 == 1), axis=1)
    senders = sent_queries.shape[0]
    mid_limit = jnp.broadcast_to(mid_len[0], (senders,))
    mid_result, mid_logsum = level_partial(
        sent_queries[:, 0], mid_cache[0, 0], mid_cache[1, 0], mid_limit, heads_here, False
    )
    leaf_keys = jnp.where(second[:, None, None], leaf_cache[0, 1][None], leaf_cache[0, 0][None])
    leaf_values = jnp.where(second[:, None, None], leaf_cache[1, 1][None], leaf_cache[1, 0][None])
    leaf_limit = jnp.where(second, leaf_len[1], leaf_len[0])
    leaf_result, leaf_logsum = level_partial(
        sent_queries[:, 1], leaf_keys, leaf_values, leaf_limit, heads_here, True
    )
    owner_out = jnp.stack([mid_result, leaf_result], axis=1)
    owner_lse = jnp.stack([mid_logsum, leaf_logsum], axis=1)
    owner_all = jnp.concatenate([owner_out, owner_lse], axis=-1)
    back_all = lax.all_to_all(owner_all, "dp", split_axis=0, concat_axis=0, tiled=True)
    back_out = back_all[..., :local_width]
    back_lse = back_all[..., local_width:]
    mid_out = back_out[mid_of, 0].reshape(tok_rows, heads_here, head_dim)
    mid_lse = back_lse[mid_of, 0].reshape(tok_rows, heads_here)
    leaf_out = back_out[leaf_owner, 1].reshape(tok_rows, heads_here, head_dim)
    leaf_lse = back_lse[leaf_owner, 1].reshape(tok_rows, heads_here)
    stacked_lse = jnp.stack([root_lse, mid_lse, leaf_lse, self_lse])
    stacked_out = jnp.stack([root_out, mid_out, leaf_out, self_out])
    overall = jnp.max(stacked_lse, axis=0)
    shares = jnp.exp(stacked_lse - overall)
    combined = jnp.sum(shares[..., None] * stacked_out, axis=0) / jnp.sum(shares, axis=0)[..., None]
    attended = combined.reshape(tok_rows, local_width).astype(jnp.bfloat16)
    projected = jnp.dot(attended, w_out, preferred_element_type=jnp.float32)
    rows_here = tok_rows // lax.axis_size("mp")
    first = lax.axis_index("mp") * rows_here
    attn_rows = lax.psum_scatter(projected, "mp", scatter_dimension=0, tiled=True)
    resid = lax.dynamic_slice_in_dim(hidden_in, first, rows_here, 0).astype(jnp.float32) + attn_rows
    ffn_rows = rms_scale(resid, ffn_gain).astype(jnp.bfloat16)
    ffn_in = lax.all_gather(ffn_rows, "mp", axis=0, tiled=True)
    logits = jnp.dot(ffn_in.astype(jnp.float32), w_router, precision=lax.Precision.HIGHEST)
    chosen = jnp.take_along_axis(logits, routes, axis=1)
    squashed = jax.nn.sigmoid(chosen)
    gates = squashed / jnp.sum(squashed, axis=1, keepdims=True)
    expert = lax.axis_index("mp")
    hit_each = routes == expert
    hit = jnp.any(hit_each, axis=1)
    gate_here = jnp.sum(jnp.where(hit_each, gates, 0.0), axis=1)
    order = jnp.cumsum(hit.astype(jnp.int32)) - 1
    capacity = 3 * TOP * tok_rows // (2 * lax.axis_size("mp"))
    slot_ids = jnp.arange(capacity, dtype=jnp.int32)
    pick_slot = (order[None, :] == slot_ids[:, None]) & hit[None, :]
    dispatch = jnp.dot(
        pick_slot.astype(jnp.bfloat16), ffn_in, preferred_element_type=jnp.float32
    ).astype(jnp.bfloat16)
    slot_gate = jnp.dot(pick_slot.astype(jnp.float32), gate_here, precision=lax.Precision.HIGHEST)
    gate_weight = w_gate[0]
    up_weight = w_up[0]
    down_weight = w_down[0]
    piece = lax.all_gather(dispatch, "dp", axis=0, tiled=True)
    gate_part = jnp.dot(piece, gate_weight, preferred_element_type=jnp.float32)
    up_part = jnp.dot(piece, up_weight, preferred_element_type=jnp.float32)
    partial_out = jnp.dot(
        (jax.nn.silu(gate_part) * up_part).astype(jnp.bfloat16),
        down_weight,
        preferred_element_type=jnp.float32,
    )
    expert_out = lax.psum_scatter(
        partial_out.astype(jnp.bfloat16), "dp", scatter_dimension=0, tiled=True
    )
    weighted = expert_out.astype(jnp.float32) * slot_gate[:, None]
    spread = jnp.dot(pick_slot.astype(jnp.float32).T, weighted, precision=lax.Precision.HIGHEST)
    mixed = lax.psum_scatter(
        spread.astype(jnp.bfloat16), "mp", scatter_dimension=0, tiled=True
    ).astype(jnp.float32)
    row_ids = first + jnp.arange(rows_here, dtype=jnp.int32)
    valid = row_ids % suffix < suffix_len[row_ids // suffix]
    return jnp.where(valid[:, None], resid + mixed, 0.0).astype(jnp.bfloat16)


def solution(mesh):
    return jax.shard_map(
        on_device,
        mesh=mesh,
        in_specs=(
            P("dp", None),
            P(),
            P(None, "mp"),
            P(None, "mp"),
            P(None, "mp"),
            P("mp", None),
            P(None, "dp", "mp"),
            P(None, "dp", None, "mp"),
            P(None, "dp", None, "mp"),
            P("dp"),
            P("dp"),
            P("dp"),
            P(),
            P("dp"),
            P(),
            P(),
            P("dp", None),
            P("mp", None, "dp"),
            P("mp", None, "dp"),
            P("mp", "dp", None),
        ),
        out_specs=P(("dp", "mp"), None),
        check_vma=False,
    )
```

profile of v0, /device:TPU:0, one launch (start us, length us, event | category | flops | bytes accessed | tf_op | source)
XLA Modules:
  0.0 436.8 jit_solution(13475134126374077228)
XLA Ops:
  7.3 1.6 fusion.30
  9.6 2.4 convolution_convert_fusion.7
  14.0 0.9 pad_maximum_fusion.1
  14.9 8.2 %all-to-all-start = ((bf16[16,2,32,256]{3,2,1,0:T(8,128)(2,1)}), bf16[16,2,32,256]{3,2,1,0:T(8,128)(2,1)}, u32[]{:S(2)}, u32[]{:S(2)}) async-start(bf16[16,2,32,256]{3,2,1,0:T(8,128)(2,1)} %pad_maximum_fusion.1), calls=%async_computation | async-start | bytes 1048576 | tf_op jit(solution)/shard_map/all_to_all | solution.py:146
  24.6 17.4 %all-reduce.2 = s32[128]{0:T(128)S(1)} all-reduce(s32[128]{0:T(128)S(1)} %dynamic-update-slice), channel_id=1, replica_groups=mesh['dp'=16,'mp'=8] {'dp'}, use_global_device_ids=true, to_apply=%add.2 | all-reduce | flops 128 | bytes 1024
  42.9 1.3 broadcast_select_fusion
  44.9 2.2 fusion.126
  47.2 2.5 convolution_convert_fusion.6
  49.7 1.2 fusion.125
  50.8 0.9 reshape.404
  51.7 0.9 reshape.403
  52.6 1.0 copy.259
  53.8 2.1 copy.294
  56.0 2.1 copy.296
  58.1 1.0 copy.295
  59.1 1.0 copy.297
  60.2 2.0 fusion.129
  62.2 1.1 fusion.127
  63.3 1.0 reshape_squeeze.19
  64.6 4.3 bitcast_reduce_fusion.1
  68.9 2.6 fusion.15
  71.6 2.7 fusion.58
  75.1 1.4 stack_reshape.23
  76.5 2.4 bitcast_reduce_fusion.2
  78.9 2.0 fusion.13
  80.9 1.8 fusion.63
  83.5 1.4 stack_reshape.22
  85.2 2.4 pad_maximum_fusion
  87.6 5.1 %all-to-all-start.1 = ((f32[16,2,32,260]{3,2,1,0:T(8,128)}), f32[16,2,32,260]{3,2,1,0:T(8,128)S(1)}, u32[]{:S(2)}, u32[]{:S(2)}) async-start(f32[16,2,32,260]{3,2,1,0:T(8,128)} %pad_maximum_fusion), calls=%async_computation.1 | async-start | bytes 3145728 | tf_op jit(solution)/shard_map/all_to_all | solution.py:164
  92.9 1.2 fusion.74
  94.3 2.8 convolution_convert_fusion.5
  97.1 1.1 reshape.405
  98.2 1.4 fusion.45
  99.6 0.9 copy.285
  100.4 1.9 copy.288
  102.3 10.9 %all-to-all-done.1 = f32[16,2,32,260]{3,2,1,0:T(8,128)S(1)} async-done(((f32[16,2,32,260]{3,2,1,0:T(8,128)}), f32[16,2,32,260]{3,2,1,0:T(8,128)S(1)}, u32[]{:S(2)}, u32[]{:S(2)}) %all-to-all-start.1) | async-done | bytes 1064992 | tf_op jit(solution)/shard_map/all_to_all | solution.py:164
  113.2 0.8 slice.82
  114.1 1.3 copy.298
  116.9 1.1 slice.84
  118.0 1.8 gather_fusion.4
  119.8 1.8 gather_fusion.5
  122.5 4.5 %fusion.124 = (bf16[1,4096,256]{2,1,0:T(8,128)(2,1)}, bf16[1,4096,256]{2,1,0:T(8,128)(2,1)}) fusion(bf16[2,4096,256]{2,1,0:T(8,128)(2,1)} %all-gather.4.cloned.1.call-done), kind=kLoop, calls=%fused_computation.185 | loop fusion | bytes 8388608 | tf_op jit(solution)/shard_map/slice | solution.py:93
  127.0 4.1 copy.253
  131.1 4.2 copy.282
  135.2 9.7 %bitcast_reduce_fusion = (f32[256,4]{0,1:T(4,128)S(1)}, f32[4,256,4096]{2,1,0:T(8,128)}) fusion(bf16[256,4,64]{0,2,1:T(8,128)(2,1)S(1)} %bitcast.190, bf16[4096,4,64]{0,2,1:T(8,128)(2,1)} %bitcast.174), kind=kOutput, calls=%fused_computation.8 | convolution fusion | flops 545258496 | bytes 19009536 | tf_op jit(solution)/shard_map/qhd,khd->qhk/dot_general | solution.py:96
  144.9 8.6 %fusion.2 = f32[256,4]{0,1:T(4,128)S(1)} fusion(f32[4,256,4096]{2,1,0:T(8,128)} %get-tuple-element.33, f32[256,4]{0,1:T(4,128)S(1)} %broadcast_maximum_fusion), kind=kLoop, calls=%fused_computation.11 | loop fusion | flops 12581888 | bytes 16785408 | tf_op jit(solution)/shard_map/reduce_sum | solution.py:101
  153.6 8.1 %fusion.54 = f32[1,256,4,64]{1,3,2,0:T(8,128)S(1)} fusion(bf16[4096,4,64]{0,2,1:T(8,128)(2,1)} %bitcast.176, f32[4,256,4096]{2,1,0:T(8,128)} %get-tuple-element.33, f32[256,4]{0,1:T(4,128)S(1)} %broadcast_maximum_fusion, f32[256,4]{0,1:T(4,128)S(1)} %fusion.2), kind=kOutput, calls=%fused_computation.71 | convolution fusion | flops 549519360 | bytes 19144704 | tf_op jit(solution)/shard_map/qhk,khd->qhd/dot_general | solution.py:102
  161.9 1.1 copy-done.11
  163.0 1.9 fusion.130
  165.0 31.7 %reduce-scatter.4.cloned.1.call-done = f32[32,2304]{1,0:T(8,128)} async-done(((f32[256,2304]{1,0:T(8,128)}), f32[32,2304]{1,0:T(8,128)}) %reduce-scatter.4.cloned.1.call-update) | async-done | bytes 294928 | tf_op jit(solution)/shard_map/reduce_scatter | solution.py:180
  196.6 1.1 multiply_reduce_fusion
  197.8 1.8 multiply_convert_fusion
  200.3 21.9 %all-gather.6.cloned.1.call-done = bf16[256,2304]{1,0:T(8,128)(2,1)} async-done(((bf16[32,2304]{1,0:T(8,128)(2,1)}), bf16[256,2304]{1,0:T(8,128)(2,1)}) %all-gather.6.cloned.1.call-update) | async-done | bytes 1179664 | tf_op jit(solution)/shard_map/all_gather | solution.py:183
  222.2 2.4 convolution_convert_fusion.4
  224.9 65.0 %all-gather.8.cloned.1.call-done = bf16[1536,2304]{1,0:T(8,128)(2,1)} async-done(((bf16[96,2304]{1,0:T(8,128)(2,1)}), bf16[1536,2304]{1,0:T(8,128)(2,1)}) %all-gather.8.cloned.1.call-update) | async-done | bytes 7077904 | tf_op jit(solution)/shard_map/all_gather | solution.py:203
  289.9 7.6 %fusion.35 = f32[1536,360]{0,1:T(8,128)} fusion(bf16[1536,2304]{1,0:T(8,128)(2,1)} %all-gather.8.cloned.1.call-done, bf16[1,2304,360]{1,2,0:T(8,128)(2,1)} %param.37), kind=kOutput, calls=%fused_computation.55 | convolution fusion | flops 2548039680 | bytes 10948608 | tf_op jit(solution)/shard_map/dot_general | solution.py:204
  297.5 13.1 %convolution_convert_fusion = bf16[1536,2304]{1,0:T(8,128)(2,1)} fusion(bf16[1,360,2304]{2,1,0:T(8,128)(2,1)S(1)} %copy-done, bf16[1536,2304]{1,0:T(8,128)(2,1)} %all-gather.8.cloned.1.call-done, f32[1536,360]{0,1:T(8,128)} %fusion.35, bf16[1,2304,360]{1,2,0:T(8,128)(2,1)} %param.38), kind=kOutput, calls=%fused_computation.12 | convolution fusion | flops 5102936064 | bytes 19685376 | tf_op jit(solution)/shard_map/dot_general | solution.py:206
  311.0 0.9 copy-done.4
  311.9 1.0 fusion.131
  312.9 3.6 gather_fusion.6
  316.9 76.4 %reduce-scatter.6.cloned.1.call-done = bf16[96,2304]{1,0:T(8,128)(2,1)} async-done(((bf16[1536,2304]{1,0:T(8,128)(2,1)}), bf16[96,2304]{1,0:T(8,128)(2,1)}) %reduce-scatter.6.cloned.1.call-update) | async-done | bytes 442384 | tf_op jit(solution)/shard_map/reduce_scatter | solution.py:211
  393.3 3.2 convolution_convert_fusion.3
  397.3 30.7 %reduce-scatter.8.cloned.1.call-done = bf16[32,2304]{1,0:T(8,128)(2,1)} async-done(((bf16[256,2304]{1,0:T(8,128)(2,1)}), bf16[32,2304]{1,0:T(8,128)(2,1)}) %reduce-scatter.8.cloned.1.call-update) | async-done | bytes 147472 | tf_op jit(solution)/shard_map/reduce_scatter | solution.py:216
  428.0 1.7 select_convert_fusion
  (135 shorter events, 13.1 us)
Async XLA Ops:
  6.5 290.9 %copy-start = (bf16[1,360,2304]{2,1,0:T(8,128)(2,1)S(1)}, bf16[1,360,2304]{2,1,0:T(8,128)(2,1)}, u32[]{:S(2)}) copy-start(bf16[1,360,2304]{2,1,0:T(8,128)(2,1)} %param.39) | copy-start | bytes 4976644
  6.5 116.0 %all-gather.4.cloned.1.call-start = ((), (), s32[]{:S(2)}) async-start(), calls=%async_computation.5 | async-start | bytes 4456448 | tf_op jit(solution)/shard_map/all_gather | solution.py:91
  9.5 3.5 copy-start.2
  11.9 0.7 copy-start.16
  12.7 10.4 %copy-start.26 = (u32[128]{0:T(128)S(1)}, u32[128]{0:T(128)}, u32[]{:S(2)}) copy-start(u32[128]{0:T(128)} %constant.214) | copy-start | bytes 1540
  12.7 11.7 %copy-start.24 = (s32[8]{0:T(128)S(1)}, s32[8]{0:T(128)}, u32[]{:S(2)}) copy-start(s32[8]{0:T(128)} %param.31) | copy-start | bytes 100
  12.7 29.3 %copy-start.3 = (s32[8]{0:T(128)S(1)}, s32[8]{0:T(128)}, u32[]{:S(2)}) copy-start(s32[8]{0:T(128)} %param.33) | copy-start | bytes 100
  12.7 29.3 %copy-start.23 = (s32[2]{0:T(128)S(1)}, s32[2]{0:T(128)}, u32[]{:S(2)}) copy-start(s32[2]{0:T(128)} %param.30) | copy-start | bytes 28
  14.0 33.2 %copy-start.6 = (bf16[256,2304]{1,0:T(8,128)(2,1)S(1)}, bf16[256,2304]{1,0:T(8,128)(2,1)}, u32[]{:S(2)}) copy-start(bf16[256,2304]{1,0:T(8,128)(2,1)} %param.20) | copy-start | bytes 3538948
  14.9 47.3 %all-to-all-start = ((bf16[16,2,32,256]{3,2,1,0:T(8,128)(2,1)}), bf16[16,2,32,256]{3,2,1,0:T(8,128)(2,1)}, u32[]{:S(2)}, u32[]{:S(2)}) async-start(bf16[16,2,32,256]{3,2,1,0:T(8,128)(2,1)} %pad_maximum_fusion.1), calls=%async_computation | async-start | bytes 1048576 | tf_op jit(solution)/shard_map/all_to_all | solution.py:146
  44.9 4.7 %copy-start.7 = (bf16[2,2,1024,256]{3,2,1,0:T(8,128)(2,1)S(1)}, bf16[2,2,1024,256]{3,2,1,0:T(8,128)(2,1)}, u32[]{:S(2)}) copy-start(bf16[2,2,1024,256]{3,2,1,0:T(8,128)(2,1)} %param.28) | copy-start | bytes 6291460
  49.7 2.1 copy-start.19
  49.7 3.9 copy-start.9
  53.8 4.2 copy-start.10
  53.8 6.4 %copy-start.18 = (bf16[8,32,4,64]{3,2,1,0:T(4,128)(2,1)S(1)}, bf16[8,32,4,64]{3,2,1,0:T(4,128)(2,1)}, u32[]{:S(2)}) copy-start(bf16[8,32,4,64]{3,2,1,0:T(4,128)(2,1)} %reshape.404) | copy-start | bytes 393220
  68.9 2.7 copy-start.14
  68.9 2.7 copy-start.15
  78.9 2.0 copy-start.13
  82.8 2.5 copy-start.8
  87.6 6.6 %copy-start.25 = (f32[2304]{0:T(1024)S(1)}, f32[2304]{0:T(1024)}, u32[]{:S(2)}) copy-start(f32[2304]{0:T(1024)} %param.21) | copy-start | bytes 27652
  87.6 25.6 %all-to-all-start.1 = ((f32[16,2,32,260]{3,2,1,0:T(8,128)}), f32[16,2,32,260]{3,2,1,0:T(8,128)S(1)}, u32[]{:S(2)}, u32[]{:S(2)}) async-start(f32[16,2,32,260]{3,2,1,0:T(8,128)} %pad_maximum_fusion), calls=%async_computation.1 | async-start | bytes 3145728 | tf_op jit(solution)/shard_map/all_to_all | solution.py:164
  92.7 104.0 %reduce-scatter.4.cloned.1.call-start = ((), (), s32[]{:S(2)}) async-start(), calls=%async_computation.6 | async-start | bytes 2654208 | tf_op jit(solution)/shard_map/reduce_scatter | solution.py:180
  131.1 4.2 copy-start.17
  153.6 8.2 %copy-start.12 = (f32[1,256,4,64]{1,3,2,0:T(8,128)S(1)}, f32[1,256,4,64]{1,3,2,0:T(8,128)}, u32[]{:S(2)}) copy-start(f32[1,256,4,64]{1,3,2,0:T(8,128)} %copy.288) | copy-start | bytes 786436
  161.7 1.3 copy-start.11
  163.0 34.8 %copy-start.22 = (f32[2304]{0:T(1024)S(1)}, f32[2304]{0:T(1024)}, u32[]{:S(2)}) copy-start(f32[2304]{0:T(1024)} %param.34) | copy-start | bytes 27652
  164.9 34.8 %copy-start.21 = (s32[256,2]{0,1:T(2,128)S(1)}, s32[256,2]{0,1:T(2,128)}, u32[]{:S(2)}) copy-start(s32[256,2]{0,1:T(2,128)} %param.36) | copy-start | bytes 6148
  164.9 57.3 %all-gather.6.cloned.1.call-start = ((), (), s32[]{:S(2)}) async-start(), calls=%async_computation.7 | async-start | bytes 1327104 | tf_op jit(solution)/shard_map/all_gather | solution.py:183
  199.6 90.3 %all-gather.8.cloned.1.call-start = ((), (), s32[]{:S(2)}) async-start(), calls=%async_computation.8 | async-start | bytes 7520256 | tf_op jit(solution)/shard_map/all_gather | solution.py:203
  224.6 168.7 %reduce-scatter.6.cloned.1.call-start = ((), (), s32[]{:S(2)}) async-start(), calls=%async_computation.9 | async-start | bytes 7520256 | tf_op jit(solution)/shard_map/reduce_scatter | solution.py:211
  310.6 1.3 copy-start.4
  310.6 1.3 copy-start.20
  310.6 117.3 %reduce-scatter.8.cloned.1.call-start = ((), (), s32[]{:S(2)}) async-start(), calls=%async_computation.10 | async-start | bytes 1327104 | tf_op jit(solution)/shard_map/reduce_scatter | solution.py:216
  312.9 116.8 %copy-start.1 = (bf16[1,360,2304]{2,1,0:T(8,128)(2,1)S(1)}, bf16[1,360,2304]{2,1,0:T(8,128)(2,1)}, u32[]{:S(2)}) copy-start(bf16[1,360,2304]{2,1,0:T(8,128)(2,1)} %param.39) | copy-start | bytes 4976644
  316.4 111.5 %copy-start.5 = (f32[32,2304]{1,0:T(8,128)S(1)}, f32[32,2304]{1,0:T(8,128)}, u32[]{:S(2)}) copy-start(f32[32,2304]{1,0:T(8,128)} %reduce-scatter.4.cloned.1.call-done) | copy-start | bytes 884740
Sparse Core Ops, SparseCore 0:
  9.6 57.6 all-gather.3
  165.0 31.5 reduce-scatter.3
  199.7 22.4 all-gather.5
  224.7 65.1 all-gather.7
  310.8 82.4 reduce-scatter.5
  396.6 31.2 reduce-scatter.7
where the time goes:
time: 444 us; the launch traced here: 437 us
  waiting for transfers between devices  237 us (53%)
  matrix products  69.9 us (16%)
  local copies, waits for them, and re-layouts  55.5 us (12%)
  other arithmetic  27.1 us (6%)
  blocking collectives  17.4 us (4%)
  between operations  15.6 us (4%)
  starting transfers between devices  13.8 us (3%)
    reduce_scatter x1, waiting for transfers between devices, on_device(): lax.psum_scatter(partial_out.astype(jnp.bfloat16), 'dp', scatter_dimensio...  76.4 us
    all_gather x1, waiting for transfers between devices, on_device(): piece = lax.all_gather(dispatch, 'dp', axis=0, tiled=True)  65 us
    reduce_scatter x1, waiting for transfers between devices, on_device(): lax.psum_scatter(projected, 'mp', scatter_dimension=0, tiled=True)  31.7 us
    reduce_scatter x1, waiting for transfers between devices, on_device(): lax.psum_scatter(spread.astype(jnp.bfloat16), 'mp', scatter_dimension=0,...  30.7 us
    all_gather x1, waiting for transfers between devices, on_device(): ffn_in = lax.all_gather(ffn_rows, 'mp', axis=0, tiled=True)  21.9 us
    unnamed x1, blocking collectives  17.4 us
    dot_general x1, matrix products, on_device(): jnp.dot((jax.nn.silu(gate_part) * up_part).astype(jnp.bfloat16), down_wei...  13.1 us
    unnamed x64, local copies, waits for them, and re-layouts  11.2 us
  transfers between devices with their start and end apart: 8, of which 6 were waited for; matrix products, arithmetic and copies ran while one was open for 18% of the time, Pallas kernels for 0%

commit v1 on v0

--- a/solution.py
+++ b/solution.py
@@ -200,7 +200,34 @@
     gate_weight = w_gate[0]
     up_weight = w_up[0]
     down_weight = w_down[0]
-    piece = lax.all_gather(dispatch, "dp", axis=0, tiled=True)
+    x_now, block_next, ready = (
+        lax.psum(1, axis_name="dp"),
+        lax.axis_index("dp"),
+        dispatch.shape[0],
+    )
+    piece = lax.dynamic_update_slice_in_dim(
+        jnp.zeros(
+            [u * x_now if j0 == 0 else u for j0, u in enumerate(dispatch.shape)], dispatch.dtype
+        ),
+        dispatch,
+        block_next * ready,
+        axis=0,
+    )
+    back = u_next = dispatch
+    for ii in tuple(range(1, x_now // 2 + 1)):
+        back = lax.ppermute(
+            back, axis_name="dp", perm=[(j0, (j0 + 1) % x_now) for j0 in range(x_now)]
+        )
+        piece = lax.dynamic_update_slice_in_dim(
+            piece, back, (block_next - ii) % x_now * ready, axis=0
+        )
+        if 2 * ii < x_now:
+            u_next = lax.ppermute(
+                u_next, axis_name="dp", perm=[(j0, (j0 - 1) % x_now) for j0 in range(x_now)]
+            )
+            piece = lax.dynamic_update_slice_in_dim(
+                piece, u_next, (block_next + ii) % x_now * ready, axis=0
+            )
     gate_part = jnp.dot(piece, gate_weight, preferred_element_type=jnp.float32)
     up_part = jnp.dot(piece, up_weight, preferred_element_type=jnp.float32)
     partial_out = jnp.dot(

time: 444 us -> 490 us (1.10)
  starting transfers between devices: 13.8 us -> 50 us
  local copies, waits for them, and re-layouts: 55.5 us -> 73.3 us
  waiting for transfers between devices: 237 us -> 224 us
    all_gather x1 -> x0, waiting for transfers between devices: 65 us -> none  [on_device(): piece = lax.all_gather(dispatch, 'dp', axis=0, tiled=True)]
    ppermute x0 -> x15, waiting for transfers between devices: none -> 55.7 us  [the longest x8 55.7 us: on_device(): lax.ppermute(back, axis_name='dp', perm=[(j0, (j0 + 1) % x_now) for j0 in...]
    ppermute x0 -> x15, starting transfers between devices: none -> 37.7 us  [the longest x7 36.1 us: on_device(): lax.ppermute(u_next, axis_name='dp', perm=[(j0, (j0 - 1) % x_now) for j0...]
    dynamic_update_slice x0 -> x15, local copies, waits for them, and re-layouts: none -> 13 us  [the longest x8 7.39 us: on_device(): lax.dynamic_update_slice_in_dim(piece, back, (block_next - ii) % x_now *...]
    unnamed x64 -> x62, local copies, waits for them, and re-layouts: 11.2 us -> 10.8 us
  transfers between devices with their start and end apart: 8 -> 22, of which waited for: 6 -> 13; matrix products, arithmetic and copies ran while one was open for 18% -> 18% of each run, Pallas kernels for 0% -> 0%
where the time goes in v1:
time: 490 us; the launch traced here: 482 us
  waiting for transfers between devices  224 us (46%)
  matrix products  73.7 us (15%)
  local copies, waits for them, and re-layouts  73.3 us (15%)
  starting transfers between devices  50 us (10%)
  other arithmetic  28.3 us (6%)
  blocking collectives  16.9 us (3%)
  between operations  15.3 us (3%)
    reduce_scatter x1, waiting for transfers between devices, on_device(): lax.psum_scatter(partial_out.astype(jnp.bfloat16), 'dp', scatter_dimensio...  72.4 us
    ppermute x8, waiting for transfers between devices, on_device(): lax.ppermute(back, axis_name='dp', perm=[(j0, (j0 + 1) % x_now) for j0 in...  55.7 us
    ppermute x7, starting transfers between devices, on_device(): lax.ppermute(u_next, axis_name='dp', perm=[(j0, (j0 - 1) % x_now) for j0...  36.1 us
    reduce_scatter x1, waiting for transfers between devices, on_device(): lax.psum_scatter(projected, 'mp', scatter_dimension=0, tiled=True)  31.9 us
    reduce_scatter x1, waiting for transfers between devices, on_device(): lax.psum_scatter(spread.astype(jnp.bfloat16), 'mp', scatter_dimension=0,...  30.7 us
    all_gather x1, waiting for transfers between devices, on_device(): ffn_in = lax.all_gather(ffn_rows, 'mp', axis=0, tiled=True)  21.9 us
    unnamed x1, blocking collectives  16.9 us
    dot_general x1, matrix products, on_device(): jnp.dot((jax.nn.silu(gate_part) * up_part).astype(jnp.bfloat16), down_wei...  13.2 us
  transfers between devices with their start and end apart: 22, of which 13 were waited for; matrix products, arithmetic and copies ran while one was open for 18% of the time, Pallas kernels for 0%

profile of v1, /device:TPU:0, one launch (start us, length us, event | category | flops | bytes accessed | tf_op | source)
XLA Modules:
  0.0 481.8 jit_solution(11550363277348511779)
XLA Ops:
  6.6 1.7 fusion.29
  8.3 2.4 convolution_convert_fusion.7
  12.2 1.3 gather_fusion.1
  14.9 8.1 %all-to-all-start = ((bf16[16,2,32,256]{3,2,1,0:T(8,128)(2,1)}), bf16[16,2,32,256]{3,2,1,0:T(8,128)(2,1)S(1)}, u32[]{:S(2)}, u32[]{:S(2)}) async-start(bf16[16,2,32,256]{3,2,1,0:T(8,128)(2,1)} %pad_maximum_fusion.1), calls=%async_computation | async-start | bytes 1048576 | tf_op jit(solution)/shard_map/all_to_all | solution.py:146
  25.3 16.9 %all-reduce.2 = s32[128]{0:T(128)S(1)} all-reduce(s32[128]{0:T(128)S(1)} %dynamic-update-slice), channel_id=1, replica_groups=mesh['dp'=16,'mp'=8] {'dp'}, use_global_device_ids=true, to_apply=%add.2 | all-reduce | flops 128 | bytes 1024
  45.1 2.2 fusion.128
  47.4 2.5 convolution_convert_fusion.6
  49.9 1.3 fusion.127
  52.0 2.1 copy.296
  56.4 2.1 copy.294
  58.5 2.1 copy.295
  61.9 2.0 fusion.131
  66.2 1.3 bitcast_reduce_fusion.2
  67.5 2.9 bitcast_reduce_fusion.1
  70.8 2.5 fusion.13
  73.2 2.1 fusion.15
  76.5 5.4 %fusion.60 = f32[16,32,4,64]{3,1,2,0:T(8,128)S(1)} fusion(f32[16,4,1024,32]{2,3,1,0:T(8,128)} %copy-done.3, f32[16,32,4]{1,2,0:T(4,128)S(1)} %get-tuple-element.28, pred[16,1024]{1,0:T(8,128)(4,1)S(1)} %iota_compare_fusion.1, pred[16]{0:T(512)(128)(4,1)S(1)} %fusion.99, bf16[1024,4,64]{0,2,1:T(8,128)(2,1)S(1)} %bitcast.189, ...), kind=kOutput, calls=%fused_computation.74 | convolution fusion | flops 281149440 | bytes 9994256 | tf_op jit(solution)/shard_map/sqhk,skhd->sqhd/dot_general | solution.py:45
  83.3 4.7 fusion.65
  88.7 1.4 stack_reshape.22
  90.1 2.5 pad_maximum_fusion
  92.6 3.7 all-to-all-start.1
  97.7 2.8 convolution_convert_fusion.5
  101.7 1.4 fusion.47
  103.9 1.9 copy.288
  105.8 11.0 %all-to-all-done.1 = f32[16,2,32,260]{3,2,1,0:T(8,128)S(1)} async-done(((f32[16,2,32,260]{3,2,1,0:T(8,128)}), f32[16,2,32,260]{3,2,1,0:T(8,128)S(1)}, u32[]{:S(2)}, u32[]{:S(2)}) %all-to-all-start.1) | async-done | bytes 1064992 | tf_op jit(solution)/shard_map/all_to_all | solution.py:164
  117.7 1.3 copy.298
  121.6 1.8 gather_fusion.4
  123.4 1.8 gather_fusion.5
  126.8 4.4 fusion.126
  131.2 4.3 copy.253
  135.6 9.7 %bitcast_reduce_fusion = (f32[256,4]{0,1:T(4,128)S(1)}, f32[4,256,4096]{2,1,0:T(8,128)}) fusion(bf16[256,4,64]{0,2,1:T(8,128)(2,1)S(1)} %bitcast.192, bf16[4096,4,64]{0,2,1:T(8,128)(2,1)} %bitcast.176), kind=kOutput, calls=%fused_computation.8 | convolution fusion | flops 545258496 | bytes 19009536 | tf_op jit(solution)/shard_map/qhd,khd->qhk/dot_general | solution.py:96
  145.3 4.2 copy.282
  149.4 8.6 %fusion.2 = f32[256,4]{0,1:T(4,128)S(1)} fusion(f32[4,256,4096]{2,1,0:T(8,128)} %get-tuple-element.33, f32[256,4]{0,1:T(4,128)S(1)} %broadcast_maximum_fusion), kind=kLoop, calls=%fused_computation.11 | loop fusion | flops 12581888 | bytes 16785408 | tf_op jit(solution)/shard_map/reduce_sum | solution.py:101
  158.1 10.2 %fusion.56 = f32[1,256,4,64]{1,3,2,0:T(8,128)} fusion(bf16[4096,4,64]{0,2,1:T(8,128)(2,1)} %bitcast.178, f32[4,256,4096]{2,1,0:T(8,128)} %get-tuple-element.33, f32[256,4]{0,1:T(4,128)S(1)} %broadcast_maximum_fusion, f32[256,4]{0,1:T(4,128)S(1)} %fusion.2), kind=kOutput, calls=%fused_computation.71 | convolution fusion | flops 549519360 | bytes 19144704 | tf_op jit(solution)/shard_map/qhk,khd->qhd/dot_general | solution.py:102
  169.6 1.9 fusion.132
  171.6 31.9 %reduce-scatter.4.cloned.1.call-done = f32[32,2304]{1,0:T(8,128)} async-done(((f32[256,2304]{1,0:T(8,128)}), f32[32,2304]{1,0:T(8,128)}) %reduce-scatter.4.cloned.1.call-update) | async-done | bytes 294928 | tf_op jit(solution)/shard_map/reduce_scatter | solution.py:180
  204.7 1.8 multiply_convert_fusion.1
  207.2 21.9 %all-gather.5.cloned.1.call-done = bf16[256,2304]{1,0:T(8,128)(2,1)} async-done(((bf16[32,2304]{1,0:T(8,128)(2,1)}), bf16[256,2304]{1,0:T(8,128)(2,1)}) %all-gather.5.cloned.1.call-update) | async-done | bytes 1179664 | tf_op jit(solution)/shard_map/all_gather | solution.py:183
  229.0 3.4 broadcast_in_dim.179
  232.4 1.3 constant_dynamic-update-slice_fusion.15
  233.7 1.6 collective-permute-start
  235.2 3.8 collective-permute-start.1
  239.0 10.7 %collective-permute-done = bf16[96,2304]{1,0:T(8,128)(2,1)} collective-permute-done((bf16[96,2304]{1,0:T(8,128)(2,1)}, bf16[96,2304]{1,0:T(8,128)(2,1)}, u32[]{:S(2)}, u32[]{:S(2)}) %collective-permute-start) | collective-permute-done | bytes 442400 | tf_op jit(solution)/shard_map/ppermute | solution.py:218
  249.7 5.6 %collective-permute-start.3 = (bf16[96,2304]{1,0:T(8,128)(2,1)S(1)}, bf16[96,2304]{1,0:T(8,128)(2,1)S(1)}, u32[]{:S(2)}, u32[]{:S(2)}) collective-permute-start(bf16[96,2304]{1,0:T(8,128)(2,1)S(1)} %collective-permute-done.1), channel_id=1, source_target_pairs={{0,120},{8,0},{16,8},{24,16},{32,24},{40,32},{48,40},{56,48},{64,5... | collective-permute-start | bytes 1327112 | tf_op jit(solution)/shard_map/ppermute | solution.py:225
  255.3 1.8 constant_dynamic-update-slice_fusion.14
  257.9 6.9 %collective-permute-done.2 = bf16[96,2304]{1,0:T(8,128)(2,1)S(1)} collective-permute-done((bf16[96,2304]{1,0:T(8,128)(2,1)}, bf16[96,2304]{1,0:T(8,128)(2,1)S(1)}, u32[]{:S(2)}, u32[]{:S(2)}) %collective-permute-start.2) | collective-permute-done | bytes 442400 | tf_op jit(solution)/shard_map/ppermute | solution.py:218
  264.8 5.3 %collective-permute-start.5 = (bf16[96,2304]{1,0:T(8,128)(2,1)S(1)}, bf16[96,2304]{1,0:T(8,128)(2,1)S(1)}, u32[]{:S(2)}, u32[]{:S(2)}) collective-permute-start(bf16[96,2304]{1,0:T(8,128)(2,1)S(1)} %collective-permute-done.3), channel_id=1, source_target_pairs={{0,120},{8,0},{16,8},{24,16},{32,24},{40,32},{48,40},{56,48},{64,5... | collective-permute-start | bytes 1327112 | tf_op jit(solution)/shard_map/ppermute | solution.py:225
  271.7 7.0 %collective-permute-done.4 = bf16[96,2304]{1,0:T(8,128)(2,1)S(1)} collective-permute-done((bf16[96,2304]{1,0:T(8,128)(2,1)S(1)}, bf16[96,2304]{1,0:T(8,128)(2,1)S(1)}, u32[]{:S(2)}, u32[]{:S(2)}) %collective-permute-start.4) | collective-permute-done | bytes 442400 | tf_op jit(solution)/shard_map/ppermute | solution.py:218
  278.7 5.3 %collective-permute-start.7 = (bf16[96,2304]{1,0:T(8,128)(2,1)S(1)}, bf16[96,2304]{1,0:T(8,128)(2,1)S(1)}, u32[]{:S(2)}, u32[]{:S(2)}) collective-permute-start(bf16[96,2304]{1,0:T(8,128)(2,1)S(1)} %collective-permute-done.5), channel_id=1, source_target_pairs={{0,120},{8,0},{16,8},{24,16},{32,24},{40,32},{48,40},{56,48},{64,5... | collective-permute-start | bytes 1327112 | tf_op jit(solution)/shard_map/ppermute | solution.py:225
  285.7 6.1 %collective-permute-done.6 = bf16[96,2304]{1,0:T(8,128)(2,1)S(1)} collective-permute-done((bf16[96,2304]{1,0:T(8,128)(2,1)S(1)}, bf16[96,2304]{1,0:T(8,128)(2,1)S(1)}, u32[]{:S(2)}, u32[]{:S(2)}) %collective-permute-start.6) | collective-permute-done | bytes 442400 | tf_op jit(solution)/shard_map/ppermute | solution.py:218
  291.8 5.3 %collective-permute-start.9 = (bf16[96,2304]{1,0:T(8,128)(2,1)S(1)}, bf16[96,2304]{1,0:T(8,128)(2,1)S(1)}, u32[]{:S(2)}, u32[]{:S(2)}) collective-permute-start(bf16[96,2304]{1,0:T(8,128)(2,1)S(1)} %collective-permute-done.7), channel_id=1, source_target_pairs={{0,120},{8,0},{16,8},{24,16},{32,24},{40,32},{48,40},{56,48},{64,5... | collective-permute-start | bytes 1327112 | tf_op jit(solution)/shard_map/ppermute | solution.py:225
  298.7 5.1 %collective-permute-done.8 = bf16[96,2304]{1,0:T(8,128)(2,1)S(1)} collective-permute-done((bf16[96,2304]{1,0:T(8,128)(2,1)S(1)}, bf16[96,2304]{1,0:T(8,128)(2,1)S(1)}, u32[]{:S(2)}, u32[]{:S(2)}) %collective-permute-start.8) | collective-permute-done | bytes 442400 | tf_op jit(solution)/shard_map/ppermute | solution.py:218
  303.9 5.3 %collective-permute-start.11 = (bf16[96,2304]{1,0:T(8,128)(2,1)S(1)}, bf16[96,2304]{1,0:T(8,128)(2,1)S(1)}, u32[]{:S(2)}, u32[]{:S(2)}) collective-permute-start(bf16[96,2304]{1,0:T(8,128)(2,1)S(1)} %collective-permute-done.9), channel_id=1, source_target_pairs={{0,120},{8,0},{16,8},{24,16},{32,24},{40,32},{48,40},{56,48},{64,5... | collective-permute-start | bytes 1327112 | tf_op jit(solution)/shard_map/ppermute | solution.py:225
  310.8 4.7 collective-permute-done.10
  315.5 5.3 %collective-permute-start.13 = (bf16[96,2304]{1,0:T(8,128)(2,1)S(1)}, bf16[96,2304]{1,0:T(8,128)(2,1)S(1)}, u32[]{:S(2)}, u32[]{:S(2)}) collective-permute-start(bf16[96,2304]{1,0:T(8,128)(2,1)S(1)} %collective-permute-done.11), channel_id=1, source_target_pairs={{0,120},{8,0},{16,8},{24,16},{32,24},{40,32},{48,40},{56,48},{64,5... | collective-permute-start | bytes 1327112 | tf_op jit(solution)/shard_map/ppermute | solution.py:225
  322.5 5.2 %collective-permute-done.12 = bf16[96,2304]{1,0:T(8,128)(2,1)S(1)} collective-permute-done((bf16[96,2304]{1,0:T(8,128)(2,1)S(1)}, bf16[96,2304]{1,0:T(8,128)(2,1)S(1)}, u32[]{:S(2)}, u32[]{:S(2)}) %collective-permute-start.12) | collective-permute-done | bytes 442400 | tf_op jit(solution)/shard_map/ppermute | solution.py:218
  329.2 10.0 %collective-permute-done.14 = bf16[96,2304]{1,0:T(8,128)(2,1)S(1)} collective-permute-done((bf16[96,2304]{1,0:T(8,128)(2,1)S(1)}, bf16[96,2304]{1,0:T(8,128)(2,1)S(1)}, u32[]{:S(2)}, u32[]{:S(2)}) %collective-permute-start.14) | collective-permute-done | bytes 442400 | tf_op jit(solution)/shard_map/ppermute | solution.py:218
  340.1 7.2 %fusion.37 = f32[1536,360]{0,1:T(8,128)} fusion(bf16[1536,2304]{1,0:T(8,128)(2,1)} %constant_dynamic-update-slice_fusion, bf16[1,2304,360]{1,2,0:T(8,128)(2,1)S(1)} %copy-done.23), kind=kOutput, calls=%fused_computation.55 | convolution fusion | flops 2548039680 | bytes 10948608 | tf_op jit(solution)/shard_map/dot_general | solution.py:231
  347.2 13.2 %convolution_convert_fusion = bf16[1536,2304]{1,0:T(8,128)(2,1)} fusion(bf16[1,360,2304]{2,1,0:T(8,128)(2,1)S(1)} %copy-done, f32[1536,360]{0,1:T(8,128)} %fusion.37, bf16[1536,2304]{1,0:T(8,128)(2,1)} %constant_dynamic-update-slice_fusion, bf16[1,2304,360]{1,2,0:T(8,128)(2,1)} %param.38), kind=kOutput, calls=%fused_computation.12 | convolution fusion | flops 5102936064 | bytes 19685376 | tf_op jit(solution)/shard_map/dot_general | solution.py:233
  362.3 3.6 gather_fusion.6
  366.3 72.4 %reduce-scatter.6.cloned.1.call-done = bf16[96,2304]{1,0:T(8,128)(2,1)} async-done(((bf16[1536,2304]{1,0:T(8,128)(2,1)}), bf16[96,2304]{1,0:T(8,128)(2,1)}) %reduce-scatter.6.cloned.1.call-update) | async-done | bytes 442384 | tf_op jit(solution)/shard_map/reduce_scatter | solution.py:238
  438.6 3.2 convolution_convert_fusion.3
  442.6 30.7 %reduce-scatter.8.cloned.1.call-done = bf16[32,2304]{1,0:T(8,128)(2,1)} async-done(((bf16[256,2304]{1,0:T(8,128)(2,1)}), bf16[32,2304]{1,0:T(8,128)(2,1)}) %reduce-scatter.8.cloned.1.call-update) | async-done | bytes 147472 | tf_op jit(solution)/shard_map/reduce_scatter | solution.py:243
  473.3 1.7 select_convert_fusion
  (176 shorter events, 42.5 us)
Async XLA Ops:
  6.5 340.7 %copy-start = (bf16[1,360,2304]{2,1,0:T(8,128)(2,1)S(1)}, bf16[1,360,2304]{2,1,0:T(8,128)(2,1)}, u32[]{:S(2)}) copy-start(bf16[1,360,2304]{2,1,0:T(8,128)(2,1)} %param.39) | copy-start | bytes 4976644
  6.5 17.2 %copy-start.25 = (u32[128]{0:T(128)S(1)}, u32[128]{0:T(128)}, u32[]{:S(2)}) copy-start(u32[128]{0:T(128)} %constant.312) | copy-start | bytes 1540
  6.5 40.8 %copy-start.6 = (bf16[256,2304]{1,0:T(8,128)(2,1)S(1)}, bf16[256,2304]{1,0:T(8,128)(2,1)}, u32[]{:S(2)}) copy-start(bf16[256,2304]{1,0:T(8,128)(2,1)} %param.20) | copy-start | bytes 3538948
  6.5 18.5 %copy-start.22 = (s32[8]{0:T(128)S(1)}, s32[8]{0:T(128)}, u32[]{:S(2)}) copy-start(s32[8]{0:T(128)} %param.31) | copy-start | bytes 100
  6.5 35.8 %copy-start.21 = (s32[2]{0:T(128)S(1)}, s32[2]{0:T(128)}, u32[]{:S(2)}) copy-start(s32[2]{0:T(128)} %param.30) | copy-start | bytes 28
  6.5 36.4 %copy-start.1 = (s32[8]{0:T(128)S(1)}, s32[8]{0:T(128)}, u32[]{:S(2)}) copy-start(s32[8]{0:T(128)} %param.33) | copy-start | bytes 100
  10.7 0.7 copy-start.15
  14.9 49.1 %all-to-all-start = ((bf16[16,2,32,256]{3,2,1,0:T(8,128)(2,1)}), bf16[16,2,32,256]{3,2,1,0:T(8,128)(2,1)S(1)}, u32[]{:S(2)}, u32[]{:S(2)}) async-start(bf16[16,2,32,256]{3,2,1,0:T(8,128)(2,1)} %pad_maximum_fusion.1), calls=%async_computation | async-start | bytes 1048576 | tf_op jit(solution)/shard_map/all_to_all | solution.py:146
  23.0 103.8 %all-gather.3.cloned.1.call-start = ((), (), s32[]{:S(2)}) async-start(), calls=%async_computation.5 | async-start | bytes 4456448 | tf_op jit(solution)/shard_map/all_gather | solution.py:91
  42.3 7.6 %copy-start.7 = (bf16[2,2,1024,256]{3,2,1,0:T(8,128)(2,1)S(1)}, bf16[2,2,1024,256]{3,2,1,0:T(8,128)(2,1)}, u32[]{:S(2)}) copy-start(bf16[2,2,1024,256]{3,2,1,0:T(8,128)(2,1)} %param.28) | copy-start | bytes 6291460
  49.9 10.7 %copy-start.8 = (bf16[1,1,1024,256]{3,2,1,0:T(8,128)(2,1)S(1)}, bf16[1,1,1024,256]{3,2,1,0:T(8,128)(2,1)}, u32[]{:S(2)}) copy-start(bf16[1,1,1024,256]{3,2,1,0:T(8,128)(2,1)} %get-tuple-element.17) | copy-start | bytes 1572868
  49.9 11.8 %copy-start.17 = (bf16[256,256]{1,0:T(8,128)(2,1)S(1)}, bf16[256,256]{1,0:T(8,128)(2,1)}, u32[]{:S(2)}) copy-start(bf16[256,256]{1,0:T(8,128)(2,1)} %convolution_convert_fusion.6) | copy-start | bytes 393220
  66.2 1.4 copy-start.13
  66.2 1.4 copy-start.14
  67.5 3.2 copy-start.2
  70.5 4.9 %copy-start.3 = (f32[16,4,1024,32]{2,3,1,0:T(8,128)}, f32[16,4,1024,32]{2,3,1,0:T(8,128)S(1)}, u32[]{:S(2)}) copy-start(f32[16,4,1024,32]{2,3,1,0:T(8,128)S(1)} %get-tuple-element.29) | copy-start | bytes 25165828
  70.7 5.7 %copy-start.11 = (bf16[1,1,1024,256]{2,3,1,0:T(8,128)(2,1)S(1)}, bf16[1,1,1024,256]{2,3,1,0:T(8,128)(2,1)}, u32[]{:S(2)}) copy-start(bf16[1,1,1024,256]{2,3,1,0:T(8,128)(2,1)} %copy.294) | copy-start | bytes 1572868
  70.7 5.7 %copy-start.12 = (bf16[1,1,1024,256]{2,3,1,0:T(8,128)(2,1)S(1)}, bf16[1,1,1024,256]{2,3,1,0:T(8,128)(2,1)}, u32[]{:S(2)}) copy-start(bf16[1,1,1024,256]{2,3,1,0:T(8,128)(2,1)} %copy.295) | copy-start | bytes 1572868
  88.0 9.8 %copy-start.24 = (f32[2304]{0:T(1024)S(1)}, f32[2304]{0:T(1024)}, u32[]{:S(2)}) copy-start(f32[2304]{0:T(1024)} %param.21) | copy-start | bytes 27652
  92.6 24.2 %all-to-all-start.1 = ((f32[16,2,32,260]{3,2,1,0:T(8,128)}), f32[16,2,32,260]{3,2,1,0:T(8,128)S(1)}, u32[]{:S(2)}, u32[]{:S(2)}) async-start(f32[16,2,32,260]{3,2,1,0:T(8,128)} %pad_maximum_fusion), calls=%async_computation.1 | async-start | bytes 3145728 | tf_op jit(solution)/shard_map/all_to_all | solution.py:164
  96.3 107.2 %reduce-scatter.4.cloned.1.call-start = ((), (), s32[]{:S(2)}) async-start(), calls=%async_computation.6 | async-start | bytes 2654208 | tf_op jit(solution)/shard_map/reduce_scatter | solution.py:180
  125.6 9.9 %copy-start.16 = (bf16[256,256]{0,1:T(8,128)(2,1)S(1)}, bf16[256,256]{0,1:T(8,128)(2,1)}, u32[]{:S(2)}) copy-start(bf16[256,256]{0,1:T(8,128)(2,1)} %copy-done.15) | copy-start | bytes 393220
  158.1 10.3 %copy-start.10 = (f32[1,256,4,64]{1,3,2,0:T(8,128)S(1)}, f32[1,256,4,64]{1,3,2,0:T(8,128)}, u32[]{:S(2)}) copy-start(f32[1,256,4,64]{1,3,2,0:T(8,128)} %copy.288) | copy-start | bytes 786436
  158.1 11.5 %copy-start.9 = (bf16[256,2304]{1,0:T(8,128)(2,1)S(1)}, bf16[256,2304]{1,0:T(8,128)(2,1)}, u32[]{:S(2)}) copy-start(bf16[256,2304]{1,0:T(8,128)(2,1)} %param.25) | copy-start | bytes 3538948
  168.3 36.4 %copy-start.20 = (f32[2304]{0:T(1024)S(1)}, f32[2304]{0:T(1024)}, u32[]{:S(2)}) copy-start(f32[2304]{0:T(1024)} %param.34) | copy-start | bytes 27652
  168.3 38.2 %copy-start.19 = (s32[256,2]{0,1:T(2,128)S(1)}, s32[256,2]{0,1:T(2,128)}, u32[]{:S(2)}) copy-start(s32[256,2]{0,1:T(2,128)} %param.36) | copy-start | bytes 6148
  171.6 57.5 %all-gather.5.cloned.1.call-start = ((), (), s32[]{:S(2)}) async-start(), calls=%async_computation.7 | async-start | bytes 1327104 | tf_op jit(solution)/shard_map/all_gather | solution.py:183
  206.5 232.2 %reduce-scatter.6.cloned.1.call-start = ((), (), s32[]{:S(2)}) async-start(), calls=%async_computation.8 | async-start | bytes 7520256 | tf_op jit(solution)/shard_map/reduce_scatter | solution.py:238
  229.0 3.4 copy-start.4
  233.7 16.0 %collective-permute-start = (bf16[96,2304]{1,0:T(8,128)(2,1)}, bf16[96,2304]{1,0:T(8,128)(2,1)}, u32[]{:S(2)}, u32[]{:S(2)}) collective-permute-start(bf16[96,2304]{1,0:T(8,128)(2,1)} %get-tuple-element.35), channel_id=1, source_target_pairs={{0,8},{8,16},{16,24},{24,32},{32,40},{40,48},{48,56},{56,64},{64,7... | collective-permute-start | bytes 1327112 | tf_op jit(solution)/shard_map/ppermute | solution.py:218
  235.2 14.4 %collective-permute-start.1 = (bf16[96,2304]{1,0:T(8,128)(2,1)}, bf16[96,2304]{1,0:T(8,128)(2,1)S(1)}, u32[]{:S(2)}, u32[]{:S(2)}) collective-permute-start(bf16[96,2304]{1,0:T(8,128)(2,1)} %get-tuple-element.35), channel_id=1, source_target_pairs={{0,120},{8,0},{16,8},{24,16},{32,24},{40,32},{48,40},{56,48},{64,5... | collective-permute-start | bytes 1327112 | tf_op jit(solution)/shard_map/ppermute | solution.py:225
  239.0 101.0 %copy-start.23 = (bf16[1,2304,360]{1,2,0:T(8,128)(2,1)S(1)}, bf16[1,2304,360]{1,2,0:T(8,128)(2,1)}, u32[]{:S(2)}) copy-start(bf16[1,2304,360]{1,2,0:T(8,128)(2,1)} %param.37) | copy-start | bytes 4976644
  249.7 15.1 %collective-permute-start.2 = (bf16[96,2304]{1,0:T(8,128)(2,1)}, bf16[96,2304]{1,0:T(8,128)(2,1)S(1)}, u32[]{:S(2)}, u32[]{:S(2)}) collective-permute-start(bf16[96,2304]{1,0:T(8,128)(2,1)} %collective-permute-done), channel_id=1, source_target_pairs={{0,8},{8,16},{16,24},{24,32},{32,40},{40,48},{48,56},{56,64},{64,7... | collective-permute-start | bytes 1327112 | tf_op jit(solution)/shard_map/ppermute | solution.py:218
  249.7 15.1 %collective-permute-start.3 = (bf16[96,2304]{1,0:T(8,128)(2,1)S(1)}, bf16[96,2304]{1,0:T(8,128)(2,1)S(1)}, u32[]{:S(2)}, u32[]{:S(2)}) collective-permute-start(bf16[96,2304]{1,0:T(8,128)(2,1)S(1)} %collective-permute-done.1), channel_id=1, source_target_pairs={{0,120},{8,0},{16,8},{24,16},{32,24},{40,32},{48,40},{56,48},{64,5... | collective-permute-start | bytes 1327112 | tf_op jit(solution)/shard_map/ppermute | solution.py:225
  264.8 14.0 %collective-permute-start.4 = (bf16[96,2304]{1,0:T(8,128)(2,1)S(1)}, bf16[96,2304]{1,0:T(8,128)(2,1)S(1)}, u32[]{:S(2)}, u32[]{:S(2)}) collective-permute-start(bf16[96,2304]{1,0:T(8,128)(2,1)S(1)} %collective-permute-done.2), channel_id=1, source_target_pairs={{0,8},{8,16},{16,24},{24,32},{32,40},{40,48},{48,56},{56,64},{64,7... | collective-permute-start | bytes 1327112 | tf_op jit(solution)/shard_map/ppermute | solution.py:218
  264.8 14.0 %collective-permute-start.5 = (bf16[96,2304]{1,0:T(8,128)(2,1)S(1)}, bf16[96,2304]{1,0:T(8,128)(2,1)S(1)}, u32[]{:S(2)}, u32[]{:S(2)}) collective-permute-start(bf16[96,2304]{1,0:T(8,128)(2,1)S(1)} %collective-permute-done.3), channel_id=1, source_target_pairs={{0,120},{8,0},{16,8},{24,16},{32,24},{40,32},{48,40},{56,48},{64,5... | collective-permute-start | bytes 1327112 | tf_op jit(solution)/shard_map/ppermute | solution.py:225
  278.7 13.0 %collective-permute-start.6 = (bf16[96,2304]{1,0:T(8,128)(2,1)S(1)}, bf16[96,2304]{1,0:T(8,128)(2,1)S(1)}, u32[]{:S(2)}, u32[]{:S(2)}) collective-permute-start(bf16[96,2304]{1,0:T(8,128)(2,1)S(1)} %collective-permute-done.4), channel_id=1, source_target_pairs={{0,8},{8,16},{16,24},{24,32},{32,40},{40,48},{48,56},{56,64},{64,7... | collective-permute-start | bytes 1327112 | tf_op jit(solution)/shard_map/ppermute | solution.py:218
  278.7 13.0 %collective-permute-start.7 = (bf16[96,2304]{1,0:T(8,128)(2,1)S(1)}, bf16[96,2304]{1,0:T(8,128)(2,1)S(1)}, u32[]{:S(2)}, u32[]{:S(2)}) collective-permute-start(bf16[96,2304]{1,0:T(8,128)(2,1)S(1)} %collective-permute-done.5), channel_id=1, source_target_pairs={{0,120},{8,0},{16,8},{24,16},{32,24},{40,32},{48,40},{56,48},{64,5... | collective-permute-start | bytes 1327112 | tf_op jit(solution)/shard_map/ppermute | solution.py:225
  291.8 12.1 %collective-permute-start.8 = (bf16[96,2304]{1,0:T(8,128)(2,1)S(1)}, bf16[96,2304]{1,0:T(8,128)(2,1)S(1)}, u32[]{:S(2)}, u32[]{:S(2)}) collective-permute-start(bf16[96,2304]{1,0:T(8,128)(2,1)S(1)} %collective-permute-done.6), channel_id=1, source_target_pairs={{0,8},{8,16},{16,24},{24,32},{32,40},{40,48},{48,56},{56,64},{64,7... | collective-permute-start | bytes 1327112 | tf_op jit(solution)/shard_map/ppermute | solution.py:218
  291.8 12.1 %collective-permute-start.9 = (bf16[96,2304]{1,0:T(8,128)(2,1)S(1)}, bf16[96,2304]{1,0:T(8,128)(2,1)S(1)}, u32[]{:S(2)}, u32[]{:S(2)}) collective-permute-start(bf16[96,2304]{1,0:T(8,128)(2,1)S(1)} %collective-permute-done.7), channel_id=1, source_target_pairs={{0,120},{8,0},{16,8},{24,16},{32,24},{40,32},{48,40},{56,48},{64,5... | collective-permute-start | bytes 1327112 | tf_op jit(solution)/shard_map/ppermute | solution.py:225
  303.9 11.6 %collective-permute-start.10 = (bf16[96,2304]{1,0:T(8,128)(2,1)S(1)}, bf16[96,2304]{1,0:T(8,128)(2,1)S(1)}, u32[]{:S(2)}, u32[]{:S(2)}) collective-permute-start(bf16[96,2304]{1,0:T(8,128)(2,1)S(1)} %collective-permute-done.8), channel_id=1, source_target_pairs={{0,8},{8,16},{16,24},{24,32},{32,40},{40,48},{48,56},{56,64},{64,7... | collective-permute-start | bytes 1327112 | tf_op jit(solution)/shard_map/ppermute | solution.py:218
  303.9 11.6 %collective-permute-start.11 = (bf16[96,2304]{1,0:T(8,128)(2,1)S(1)}, bf16[96,2304]{1,0:T(8,128)(2,1)S(1)}, u32[]{:S(2)}, u32[]{:S(2)}) collective-permute-start(bf16[96,2304]{1,0:T(8,128)(2,1)S(1)} %collective-permute-done.9), channel_id=1, source_target_pairs={{0,120},{8,0},{16,8},{24,16},{32,24},{40,32},{48,40},{56,48},{64,5... | collective-permute-start | bytes 1327112 | tf_op jit(solution)/shard_map/ppermute | solution.py:225
  315.5 12.1 %collective-permute-start.12 = (bf16[96,2304]{1,0:T(8,128)(2,1)S(1)}, bf16[96,2304]{1,0:T(8,128)(2,1)S(1)}, u32[]{:S(2)}, u32[]{:S(2)}) collective-permute-start(bf16[96,2304]{1,0:T(8,128)(2,1)S(1)} %collective-permute-done.10), channel_id=1, source_target_pairs={{0,8},{8,16},{16,24},{24,32},{32,40},{40,48},{48,56},{56,64},{64,7... | collective-permute-start | bytes 1327112 | tf_op jit(solution)/shard_map/ppermute | solution.py:218
  315.5 12.9 %collective-permute-start.13 = (bf16[96,2304]{1,0:T(8,128)(2,1)S(1)}, bf16[96,2304]{1,0:T(8,128)(2,1)S(1)}, u32[]{:S(2)}, u32[]{:S(2)}) collective-permute-start(bf16[96,2304]{1,0:T(8,128)(2,1)S(1)} %collective-permute-done.11), channel_id=1, source_target_pairs={{0,120},{8,0},{16,8},{24,16},{32,24},{40,32},{48,40},{56,48},{64,5... | collective-permute-start | bytes 1327112 | tf_op jit(solution)/shard_map/ppermute | solution.py:225
  327.6 11.6 %collective-permute-start.14 = (bf16[96,2304]{1,0:T(8,128)(2,1)S(1)}, bf16[96,2304]{1,0:T(8,128)(2,1)S(1)}, u32[]{:S(2)}, u32[]{:S(2)}) collective-permute-start(bf16[96,2304]{1,0:T(8,128)(2,1)S(1)} %collective-permute-done.12), channel_id=1, source_target_pairs={{0,8},{8,16},{16,24},{24,32},{32,40},{40,48},{48,56},{56,64},{64,7... | collective-permute-start | bytes 1327112 | tf_op jit(solution)/shard_map/ppermute | solution.py:218
  360.4 0.9 copy-start.18
  360.4 112.9 %reduce-scatter.8.cloned.1.call-start = ((), (), s32[]{:S(2)}) async-start(), calls=%async_computation.9 | async-start | bytes 1327104 | tf_op jit(solution)/shard_map/reduce_scatter | solution.py:243
  362.3 111.0 %copy-start.5 = (f32[32,2304]{1,0:T(8,128)S(1)}, f32[32,2304]{1,0:T(8,128)}, u32[]{:S(2)}) copy-start(f32[32,2304]{1,0:T(8,128)} %reduce-scatter.4.cloned.1.call-done) | copy-start | bytes 884740
Sparse Core Ops, SparseCore 0:
  26.1 53.2 all-gather.2
  171.7 31.7 reduce-scatter.3
  206.6 22.4 all-gather.4
  360.6 78.0 reduce-scatter.5
  442.0 31.2 reduce-scatter.7
